TPU v7x, 256 devices: a whole 4x4x8 slice. The times are simulated.
256 devices in a mesh: island: 8 (over y_lo, x), fsdp: 32 (over z, y_hi, core).
Axes of the slice: x: 4, y: 4 (y_hi: 2, y_lo: 2; y = y_hi * 2 + y_lo), z: 8, core: 2. Of those that a mesh axis runs over, the one named last changes fastest.
Arguments:
- global_params: bfloat16 [8, 1, 4096, 8192], P('island', None, 'fsdp'), may hold values from -6 to 6
- local_params: bfloat16 [8, 1, 4096, 8192], P('island', None, 'fsdp'), may hold values from -6 to 6
- momentum: bfloat16 [8, 1, 4096, 8192], P('island', None, 'fsdp'), may hold values from -6 to 6
- init_factors: float32 [4, 1, 4, 8192], replicated, may hold values from -6 to 6
- seeds: int32 [8], replicated, may hold values from 0 to 3, as said below
- plan: int32 [8], replicated, may hold values from 1 to 4, as said below
- round_index: int32 [], replicated, may hold values from 0 to 999
Outputs:
- new_params: bfloat16 [8, 1, 4096, 8192], P('island', None, 'fsdp')
- new_momentum: bfloat16 [8, 1, 4096, 8192], P('island', None, 'fsdp')
- warm_factors: float32 [8, 1, 4, 8192], P('island')
Inputs may be any that keep to these rules, and one draw needn't show every extreme that they name: `plan`: every entry is a power of two; every power of two up to 4 appears. `seeds`: every value from 0 to 3 is used by some replica.
All inputs are finite; a program needn't handle non-finite values.
Results may differ from a plain program's by a relative error of at most 0.0017.
Values sent between devices are 32-bit elements; how exact they have to be, the bound alone decides.
No kernel may reach another device: no remote copies, remote signals or barrier semaphores. Data moves between devices by JAX's collectives and lax.ppermute only.
A program may use at most 64 MiB of HBM per device.

v0:
```python
import jax
import jax.numpy as jnp
from jax import lax
from jax.sharding import PartitionSpec as P

ITERS = 3


def swapped(x, axis, apart):
    return lax.ppermute(x, axis, [(i, i ^ 1 << apart) for i in range(lax.axis_size(axis))])


def on_device(global_params, local_params, momentum, init_factors, seeds, plan, round_index):
    high = lax.Precision.HIGHEST
    offset = plan[jnp.mod(round_index, plan.shape[0])]
    island_pos = lax.axis_index("island")
    partner = jnp.bitwise_xor(island_pos, offset)
    factor = init_factors[seeds[jnp.minimum(island_pos, partner)]]
    start = global_params[0].astype(jnp.float32)
    delta = start - local_params[0].astype(jnp.float32)
    levels = lax.axis_size("island").bit_length() - 1
    level_ids = jnp.arange(levels, dtype=jnp.int32)
    which_bit = jnp.sum(jnp.where(jnp.left_shift(jnp.int32(1), level_ids) == offset, level_ids, 0))

    def make_branch(level):

        def one_level(values):
            return swapped(values, "island", level)

        return one_level

    def from_peer(values):
        branches = [make_branch(level) for level in range(levels)]
        return lax.switch(which_bit, branches, values)

    basis = None
    for turn in range(ITERS):
        mine_left = jnp.einsum("mkc,mrc->mkr", factor, delta, precision=high)
        left = mine_left - from_peer(mine_left)
        gram_part = jnp.einsum("mkr,mjr->mkj", left, left, precision=high)
        gram = lax.psum(gram_part, "fsdp")
        lower = jnp.linalg.cholesky(gram)
        basis = lax.linalg.triangular_solve(lower, left, left_side=True, lower=True)
        right_part = jnp.einsum("mkr,mrc->mkc", basis, delta, precision=high)
        mine_right = lax.psum(right_part, "fsdp")
        factor = mine_right + from_peer(mine_right)
    correction = jnp.einsum("mkr,mkc->mrc", basis, factor, precision=high)
    gossiped = delta - 0.5 * correction
    velocity = 0.9 * momentum[0].astype(jnp.float32) + gossiped
    updated = start - 0.7 * (gossiped + 0.9 * velocity)
    return (updated.astype(jnp.bfloat16)[None], velocity.astype(jnp.bfloat16)[None], factor[None])


def solution(mesh):
    return jax.shard_map(
        on_device,
        mesh=mesh,
        in_specs=(
            P("island", None, "fsdp", None),
            P("island", None, "fsdp", None),
            P("island", None, "fsdp", None),
            P(),
            P(),
            P(),
            P(),
        ),
        out_specs=(
            P("island", None, "fsdp", None),
            P("island", None, "fsdp", None),
            P("island", None, None, None),
        ),
        check_vma=False,
    )
```

profile of v0, /device:TPU:2, one launch (start us, length us, event | category | flops | bytes accessed | tf_op | source)
XLA Modules:
  0.0 1050.5 jit_solution(16679805387560155915)
XLA Ops:
  7.9 1.2 dynamic_slice.9
  9.8 1.3 fusion.62
  11.1 1.2 dynamic_slice.10
  15.0 5.2 fusion.17
  20.1 5.2 conditional.6
  20.1 2.2 collective-permute-start.1
  22.3 3.1 collective-permute-done.1
  25.4 0.9 convolution_bitcast_fusion.5
  26.3 71.8 %psum.69 = f32[1,4,4]{1,2,0:T(4,128)S(1)} all-reduce(f32[1,4,4]{1,2,0:T(4,128)S(1)} %convolution_bitcast_fusion.5), channel_id=1, replica_groups=mesh['island'=8,'fsdp'=32] {'fsdp'}, use_global_device_ids=true, to_apply=%region_4.5 | all-reduce | flops 16 | bytes 128 | tf_op jit(solution)/shard_map/psum | solution.py:41
  98.5 0.6 compare_reduce_fusion.2
  99.2 0.6 fusion.34
  100.2 0.9 fusion.41
  101.1 4.7 convolution_bitcast_fusion.2
  105.8 243.2 %all-reduce.4.cloned.1.call-done = f32[1,4,8192]{2,1,0:T(4,128)} async-done(((f32[1,4,8192]{2,1,0:T(4,128)}), f32[1,4,8192]{2,1,0:T(4,128)}) %all-reduce.4.cloned.1.call-update) | async-done | bytes 131088 | tf_op jit(solution)/shard_map/psum | solution.py:45
  349.0 6.8 conditional.7
  349.0 2.1 collective-permute-start.4
  351.1 4.7 collective-permute-done.4
  355.8 5.1 fusion.20
  360.9 5.2 conditional.8
  360.9 2.1 collective-permute-start.7
  362.9 3.1 collective-permute-done.7
  366.1 0.9 convolution_bitcast_fusion.4
  366.9 65.5 %psum.71 = f32[1,4,4]{1,2,0:T(4,128)S(1)} all-reduce(f32[1,4,4]{1,2,0:T(4,128)S(1)} %convolution_bitcast_fusion.4), channel_id=1, replica_groups=mesh['island'=8,'fsdp'=32] {'fsdp'}, use_global_device_ids=true, to_apply=%region_14.17 | all-reduce | flops 16 | bytes 128 | tf_op jit(solution)/shard_map/psum | solution.py:41
  432.6 0.4 custom-call.12
  433.0 0.6 compare_reduce_fusion.1
  433.6 0.6 fusion.35
  434.6 0.9 fusion.39
  435.5 4.7 convolution_bitcast_fusion.1
  440.2 247.2 %all-reduce.6.cloned.1.call-done = f32[1,4,8192]{2,1,0:T(4,128)} async-done(((f32[1,4,8192]{2,1,0:T(4,128)}), f32[1,4,8192]{2,1,0:T(4,128)}) %all-reduce.6.cloned.1.call-update) | async-done | bytes 131088 | tf_op jit(solution)/shard_map/psum | solution.py:45
  687.4 6.8 conditional.9
  687.4 2.1 collective-permute-start.10
  689.5 4.7 collective-permute-done.10
  694.2 5.1 fusion.23
  699.3 5.2 conditional.10
  699.3 2.1 collective-permute-start.13
  701.4 3.1 collective-permute-done.13
  704.5 0.9 convolution_bitcast_fusion.3
  705.4 65.5 %psum.73 = f32[1,4,4]{1,2,0:T(4,128)S(1)} all-reduce(f32[1,4,4]{1,2,0:T(4,128)S(1)} %convolution_bitcast_fusion.3), channel_id=1, replica_groups=mesh['island'=8,'fsdp'=32] {'fsdp'}, use_global_device_ids=true, to_apply=%region_22.25 | all-reduce | flops 16 | bytes 128 | tf_op jit(solution)/shard_map/psum | solution.py:41
  771.4 0.6 compare_reduce_fusion
  772.1 0.6 fusion.36
  773.1 0.9 fusion.37
  773.9 4.7 convolution_bitcast_fusion
  778.6 247.3 %all-reduce.8.cloned.1.call-done = f32[1,4,8192]{2,1,0:T(4,128)} async-done(((f32[1,4,8192]{2,1,0:T(4,128)}), f32[1,4,8192]{2,1,0:T(4,128)}) %all-reduce.8.cloned.1.call-update) | async-done | bytes 131088 | tf_op jit(solution)/shard_map/psum | solution.py:45
  1025.9 6.8 conditional.11
  1025.9 2.1 collective-permute-start.16
  1028.0 4.7 collective-permute-done.16
  1032.7 1.7 add_bitcast_fusion
  1034.4 9.6 fusion.15
  (24 shorter events, 2.3 us)
Async XLA Ops:
  7.2 7.8 copy-start
  7.2 341.8 %all-reduce.4.cloned.1.call-start = ((), (), s32[]{:S(2)}) async-start(), calls=%async_computation | async-start | bytes 262144 | tf_op jit(solution)/shard_map/psum | solution.py:45
  15.0 86.1 %copy-start.1 = (bf16[1,1,128,8192]{3,2,1,0:T(8,128)(2,1)S(1)}, bf16[1,1,128,8192]{3,2,1,0:T(8,128)(2,1)}, u32[]{:S(2)}) copy-start(bf16[1,1,128,8192]{3,2,1,0:T(8,128)(2,1)} %param.28) | copy-start | bytes 6291460
  20.1 5.2 collective-permute-start.1
  105.8 581.7 %all-reduce.6.cloned.1.call-start = ((), (), s32[]{:S(2)}) async-start(), calls=%async_computation.1 | async-start | bytes 262144 | tf_op jit(solution)/shard_map/psum | solution.py:45
  349.0 6.8 collective-permute-start.4
  360.9 5.2 collective-permute-start.7
  440.2 585.7 %all-reduce.8.cloned.1.call-start = ((), (), s32[]{:S(2)}) async-start(), calls=%async_computation.2 | async-start | bytes 262144 | tf_op jit(solution)/shard_map/psum | solution.py:45
  687.4 6.8 collective-permute-start.10
  699.3 5.2 collective-permute-start.13
  1025.9 6.8 collective-permute-start.16
Sparse Core Ops, SparseCore 0:
  105.9 243.0 all-reduce.3
  440.3 247.1 all-reduce.5
  778.8 247.1 all-reduce.7
where the time goes:
time: 1050 us
  waiting for transfers between devices  761 us (72%)
  blocking collectives  203 us (19%)
  matrix products  44.2 us (4%)
  between operations  17.8 us (2%)
  starting transfers between devices  12.7 us (1%)
    psum x3, waiting for transfers between devices, on_device(): mine_right = lax.psum(right_part, 'fsdp')  738 us
    psum x3, blocking collectives, on_device(): gram = lax.psum(gram_part, 'fsdp')  203 us
    ppermute x6, waiting for transfers between devices, swapped(): lax.ppermute(x, axis, [(i, i ^ 1 << apart) for i in range(lax.axis_size(a...  23.4 us
  transfers between devices with their start and end apart: 9, of which 9 were waited for; matrix products, arithmetic and copies ran while one was open for 0% of the time, Pallas kernels for 0%

commit v1 on v0

--- a/solution.py
+++ b/solution.py
@@ -38,7 +38,8 @@
         mine_left = jnp.einsum("mkc,mrc->mkr", factor, delta, precision=high)
         left = mine_left - from_peer(mine_left)
         gram_part = jnp.einsum("mkr,mjr->mkj", left, left, precision=high)
-        gram = lax.psum(gram_part, "fsdp")
+        parts = lax.all_gather(gram_part, "fsdp")
+        gram = jnp.sum(parts, axis=0)
         lower = jnp.linalg.cholesky(gram)
         basis = lax.linalg.triangular_solve(lower, left, left_side=True, lower=True)
         right_part = jnp.einsum("mkr,mrc->mkc", basis, delta, precision=high)

time: 1050 us -> 971 us (0.925)
  blocking collectives: 203 us -> 119 us
    psum x3 -> x0, blocking collectives: 203 us -> none  [on_device(): gram = lax.psum(gram_part, 'fsdp')]
    all_gather x0 -> x3, blocking collectives: none -> 119 us  [on_device(): parts = lax.all_gather(gram_part, 'fsdp')]
where the time goes in v1:
time: 971 us
  waiting for transfers between devices  765 us (79%)
  blocking collectives  119 us (12%)
  matrix products  44.2 us (5%)
  between operations  17.8 us (2%)
  starting transfers between devices  12.8 us (1%)
    psum x3, waiting for transfers between devices, on_device(): mine_right = lax.psum(right_part, 'fsdp')  742 us
    all_gather x3, blocking collectives, on_device(): parts = lax.all_gather(gram_part, 'fsdp')  119 us
    ppermute x6, waiting for transfers between devices, swapped(): lax.ppermute(x, axis, [(i, i ^ 1 << apart) for i in range(lax.axis_size(a...  23.4 us
  transfers between devices with their start and end apart: 9, of which 9 were waited for; matrix products, arithmetic and copies ran while one was open for 0% of the time, Pallas kernels for 0%

profile of v1, /device:TPU:2, one launch (start us, length us, event | category | flops | bytes accessed | tf_op | source)
XLA Modules:
  0.0 970.7 jit_solution(10544233522459926555)
XLA Ops:
  7.9 1.2 dynamic_slice.9
  9.8 1.3 fusion.62
  11.1 1.2 dynamic_slice.10
  15.0 5.2 fusion.17
  20.1 5.2 conditional.6
  20.1 2.2 collective-permute-start.1
  22.3 3.1 collective-permute-done.1
  25.4 0.9 convolution_bitcast_fusion.5
  26.3 45.0 %all-gather.3 = f32[32,4,4]{2,1,0:T(4,128)S(1)} all-gather(f32[1,4,4]{2,1,0:T(4,128)S(1)} %convolution_bitcast_fusion.5), channel_id=2, replica_groups=mesh['island'=8,'fsdp'=32] {'fsdp'}, dimensions={0}, use_global_device_ids=true | all-gather | bytes 2112 | tf_op jit(solution)/shard_map/all_gather | solution.py:41
  71.8 0.6 compare_reduce_fusion.2
  72.5 0.6 fusion.34
  73.5 0.9 fusion.41
  74.3 4.7 convolution_bitcast_fusion.2
  79.1 244.4 %all-reduce.4.cloned.1.call-done = f32[1,4,8192]{2,1,0:T(4,128)} async-done(((f32[1,4,8192]{2,1,0:T(4,128)}), f32[1,4,8192]{2,1,0:T(4,128)}) %all-reduce.4.cloned.1.call-update) | async-done | bytes 131088 | tf_op jit(solution)/shard_map/psum | solution.py:46
  323.5 6.8 conditional.7
  323.5 2.1 collective-permute-start.4
  325.6 4.7 collective-permute-done.4
  330.3 5.1 fusion.20
  335.4 5.4 conditional.8
  335.5 2.2 collective-permute-start.7
  337.7 3.1 collective-permute-done.7
  340.8 0.9 convolution_bitcast_fusion.4
  341.7 36.8 %all-gather.4 = f32[32,4,4]{2,1,0:T(4,128)S(1)} all-gather(f32[1,4,4]{2,1,0:T(4,128)S(1)} %convolution_bitcast_fusion.4), channel_id=3, replica_groups=mesh['island'=8,'fsdp'=32] {'fsdp'}, dimensions={0}, use_global_device_ids=true | all-gather | bytes 2112 | tf_op jit(solution)/shard_map/all_gather | solution.py:41
  378.6 0.4 custom-call.12
  379.0 0.6 compare_reduce_fusion.1
  379.7 0.6 fusion.35
  380.7 0.9 fusion.39
  381.5 4.7 convolution_bitcast_fusion.1
  386.3 248.7 %all-reduce.6.cloned.1.call-done = f32[1,4,8192]{2,1,0:T(4,128)} async-done(((f32[1,4,8192]{2,1,0:T(4,128)}), f32[1,4,8192]{2,1,0:T(4,128)}) %all-reduce.6.cloned.1.call-update) | async-done | bytes 131088 | tf_op jit(solution)/shard_map/psum | solution.py:46
  635.0 6.8 conditional.9
  635.0 2.1 collective-permute-start.10
  637.1 4.7 collective-permute-done.10
  641.8 5.1 fusion.23
  646.9 5.2 conditional.10
  646.9 2.1 collective-permute-start.13
  649.0 3.1 collective-permute-done.13
  652.1 0.9 convolution_bitcast_fusion.3
  653.0 37.0 %all-gather.5 = f32[32,4,4]{2,1,0:T(4,128)S(1)} all-gather(f32[1,4,4]{2,1,0:T(4,128)S(1)} %convolution_bitcast_fusion.3), channel_id=4, replica_groups=mesh['island'=8,'fsdp'=32] {'fsdp'}, dimensions={0}, use_global_device_ids=true | all-gather | bytes 2112 | tf_op jit(solution)/shard_map/all_gather | solution.py:41
  690.5 0.6 compare_reduce_fusion
  691.2 0.6 fusion.36
  692.2 0.9 fusion.37
  693.1 4.7 convolution_bitcast_fusion
  697.8 248.4 %all-reduce.8.cloned.1.call-done = f32[1,4,8192]{2,1,0:T(4,128)} async-done(((f32[1,4,8192]{2,1,0:T(4,128)}), f32[1,4,8192]{2,1,0:T(4,128)}) %all-reduce.8.cloned.1.call-update) | async-done | bytes 131088 | tf_op jit(solution)/shard_map/psum | solution.py:46
  946.1 6.8 conditional.11
  946.1 2.1 collective-permute-start.16
  948.2 4.7 collective-permute-done.16
  952.9 1.7 add_bitcast_fusion
  954.6 9.6 fusion.15
  (27 shorter events, 2.4 us)
Async XLA Ops:
  7.2 7.8 copy-start
  7.2 316.3 %all-reduce.4.cloned.1.call-start = ((), (), s32[]{:S(2)}) async-start(), calls=%async_computation | async-start | bytes 262144 | tf_op jit(solution)/shard_map/psum | solution.py:46
  15.0 59.4 %copy-start.1 = (bf16[1,1,128,8192]{3,2,1,0:T(8,128)(2,1)S(1)}, bf16[1,1,128,8192]{3,2,1,0:T(8,128)(2,1)}, u32[]{:S(2)}) copy-start(bf16[1,1,128,8192]{3,2,1,0:T(8,128)(2,1)} %param.28) | copy-start | bytes 6291460
  20.1 5.2 collective-permute-start.1
  79.0 556.0 %all-reduce.6.cloned.1.call-start = ((), (), s32[]{:S(2)}) async-start(), calls=%async_computation.1 | async-start | bytes 262144 | tf_op jit(solution)/shard_map/psum | solution.py:46
  323.5 6.8 collective-permute-start.4
  335.5 5.3 collective-permute-start.7
  386.2 559.9 %all-reduce.8.cloned.1.call-start = ((), (), s32[]{:S(2)}) async-start(), calls=%async_computation.2 | async-start | bytes 262144 | tf_op jit(solution)/shard_map/psum | solution.py:46
  635.0 6.8 collective-permute-start.10
  646.9 5.2 collective-permute-start.13
  946.1 6.8 collective-permute-start.16
Sparse Core Ops, SparseCore 0:
  79.1 244.3 all-reduce.3
  386.3 248.6 all-reduce.5
  697.9 248.1 all-reduce.7
